TPU v7x, 32 devices: a whole 2x2x4 slice. The times are simulated.
32 devices in a mesh: dp: 4 (over z), tensor: 8 (over y, x, core).
Axes of the slice: x: 2, y: 2, z: 4, core: 2. Of those that a mesh axis runs over, the one named last changes fastest.
Arguments:
- teacher_hidden: bfloat16 [64, 5120], P('dp', 'tensor'), may hold values from -200 to 200
- student_hidden: bfloat16 [64, 4096], P('dp', 'tensor'), may hold values from -8 to 8
- teacher_head: bfloat16 [5120, 8192], P(None, ('dp', 'tensor')), may hold values from -6 to 6
- student_head: bfloat16 [4096, 8192], P(None, ('dp', 'tensor')), may hold values from -6 to 6
- teacher_gain: float32 [5120], replicated, may hold values from 0.5 to 1.5
- lengths: int32 [8], replicated, may hold values from 1 to 8, as said below
- student_row: int32 [64], replicated, may hold values from 0 to 63, as said below
- targets: int32 [64], replicated, may hold values from 0 to 8191
Outputs:
- grad_logits: bfloat16 [64, 8192], P(None, ('dp', 'tensor'))
- divergence: float32 [64], P('dp')
- log_ratio: float32 [64], P('dp')
Inputs may be any that keep to these rules, and one draw needn't show every extreme that they name: The lengths of the 2 responses of one index of dp sum to at most 8, and to exactly 8 on some index. `student_row`: a permutation: every row of student_hidden is named once.
All inputs are finite; a program needn't handle non-finite values.
Results may differ from a plain program's by a relative error of at most 0.01095.
Values may be sent and summed in bfloat16 or wider, within the bound.
A program may use at most 64 MiB of HBM per device.

v0:
```python
import jax
import jax.numpy as jnp
from jax import lax
from jax.sharding import PartitionSpec as P

SLOT = 8


def merged_2(array, axis, combine):
    everything = jax.tree.map(lambda part: lax.all_gather(part, axis), array)
    initial = jax.tree.map(lambda part: part[0], everything)

    def turn(k, so_far):
        return combine(so_far, jax.tree.map(lambda part: part[k], everything))

    return lax.fori_loop(1, lax.axis_size(axis), turn, initial)


def on_device(
    teacher_hidden,
    student_hidden,
    teacher_head,
    student_head,
    teacher_gain,
    lengths,
    student_row,
    targets,
):
    dp_count = lax.axis_size("dp")
    tensor_count = lax.axis_size("tensor")
    local_tokens = teacher_hidden.shape[0]
    token_count = local_tokens * dp_count
    vocab_local = teacher_head.shape[1]
    dp_index = lax.axis_index("dp")
    vocab_start = (dp_index * tensor_count + lax.axis_index("tensor")) * vocab_local
    token_ids = jnp.arange(token_count, dtype=jnp.int32)
    live_all = (token_ids % SLOT < lengths[token_ids // SLOT]).astype(jnp.float32)
    teacher_full, student_full = (
        lax.all_gather(teacher_hidden, "tensor", axis=1, tiled=True),
        lax.all_gather(student_hidden, "tensor", axis=1, tiled=True),
    )
    values = lax.all_gather(teacher_full, "dp", axis=0, tiled=True).astype(jnp.float32)
    row_scale = lax.rsqrt(jnp.mean(values * values, axis=1, keepdims=True) + 1e-06)
    normed = (values * row_scale * teacher_gain[None, :]).astype(jnp.bfloat16)
    teacher_logits = jnp.dot(normed, teacher_head, preferred_element_type=jnp.float32)
    student_all = lax.all_gather(student_full, "dp", axis=0, tiled=True)
    chosen_rows = student_all[student_row[token_ids]]
    student_logits = jnp.dot(chosen_rows, student_head, preferred_element_type=jnp.float32)
    target_local = targets[token_ids] - vocab_start
    target_hits = (
        target_local[:, None] == jnp.arange(vocab_local, dtype=jnp.int32)[None, :]
    ).astype(jnp.float32)
    target_teacher = jnp.sum(target_hits * teacher_logits, axis=1)
    target_student = jnp.sum(target_hits * student_logits, axis=1)
    teacher_max = jnp.max(teacher_logits, axis=1)
    student_max = jnp.max(student_logits, axis=1)
    teacher_exp = jnp.exp(teacher_logits - teacher_max[:, None])
    student_exp = jnp.exp(student_logits - student_max[:, None])
    cross_sum = jnp.sum(student_exp * (student_logits - teacher_logits), axis=1)

    def combine(earlier, later):
        top_teacher = jnp.maximum(earlier[0], later[0])
        teacher_total = earlier[1] * jnp.exp(earlier[0] - top_teacher) + later[1] * jnp.exp(
            later[0] - top_teacher
        )
        top_student = jnp.maximum(earlier[2], later[2])
        early_rescale = jnp.exp(earlier[2] - top_student)
        late_rescale = jnp.exp(later[2] - top_student)
        return (
            top_teacher,
            teacher_total,
            top_student,
            earlier[3] * early_rescale + later[3] * late_rescale,
            earlier[4] * early_rescale + later[4] * late_rescale,
            earlier[5] + later[5],
            earlier[6] + later[6],
        )

    merged = merged_2(
        (
            teacher_max,
            jnp.sum(teacher_exp, axis=1),
            student_max,
            jnp.sum(student_exp, axis=1),
            cross_sum,
            target_teacher,
            target_student,
        ),
        ("dp", "tensor"),
        combine,
    )
    teacher_lse = merged[0] + jnp.log(merged[1])
    student_lse = merged[2] + jnp.log(merged[3])
    teacher_logp = teacher_logits - teacher_lse[:, None]
    student_logp = student_logits - student_lse[:, None]
    student_prob = jnp.exp(student_logp)
    kl_raw = merged[4] / merged[3] - student_lse + teacher_lse
    picked_teacher = merged[5]
    picked_student = merged[6]
    gradient = (
        live_all[:, None] * student_prob * (student_logp - teacher_logp - kl_raw[:, None])
    ).astype(jnp.bfloat16)
    kl_rows = live_all * kl_raw
    ratio_rows = live_all * (picked_student - student_lse - (picked_teacher - teacher_lse))
    divergence = lax.dynamic_slice_in_dim(kl_rows, dp_index * local_tokens, local_tokens)
    log_ratio = lax.dynamic_slice_in_dim(ratio_rows, dp_index * local_tokens, local_tokens)
    return (gradient, divergence, log_ratio)


def solution(mesh):
    return jax.shard_map(
        on_device,
        mesh=mesh,
        in_specs=(
            P("dp", "tensor"),
            P("dp", "tensor"),
            P(None, ("dp", "tensor")),
            P(None, ("dp", "tensor")),
            P(),
            P(),
            P(),
            P(),
        ),
        out_specs=(P(None, ("dp", "tensor")), P("dp"), P("dp")),
        check_vma=False,
    )
```

profile of v0, /device:TPU:0, one launch (start us, length us, event | category | flops | bytes accessed | tf_op | source)
XLA Modules:
  0.0 115.9 jit_solution(16936663235237315496)
XLA Ops:
  0.6 0.0 copy-start
  0.6 0.0 copy-start.3
  0.7 1.6 %gather_fusion.2 = s32[64]{0:T(128)S(1)} fusion(s32[64]{0:T(128)} %param.17, s32[1024]{0:T(1024)S(1)} %pad_clamp_fusion.1), kind=kCustom, calls=%fused_computation.2 | custom fusion | bytes 768 | tf_op jit(solution)/shard_map/gather | solution.py:49
  2.3 11.0 %all_gather.56 = bf16[16,5120]{1,0:T(8,128)(2,1)S(1)} all-gather(bf16[16,640]{1,0:T(8,128)(2,1)} %param.10), channel_id=1, replica_groups=mesh['dp'=4,'tensor'=8] {'tensor'}, dimensions={1}, use_global_device_ids=true | all-gather | bytes 184320 | tf_op jit(solution)/shard_map/all_gather | solution.py:39
  13.2 18.4 %all_gather.57 = bf16[64,5120]{1,0:T(8,128)(2,1)S(1)} all-gather(bf16[16,5120]{1,0:T(8,128)(2,1)S(1)} %all_gather.56), channel_id=1, replica_groups=mesh['dp'=4,'tensor'=8] {'dp'}, dimensions={0}, use_global_device_ids=true | all-gather | bytes 819200 | tf_op jit(solution)/shard_map/all_gather | solution.py:42
  31.6 0.0 copy-start.1
  31.6 0.2 fusion.17
  31.8 0.0 copy-start.4
  31.9 0.0 copy-done
  31.9 0.0 copy-done.3
  31.9 0.7 fusion.32
  32.6 0.0 copy-done.1
  32.6 0.8 gather_fusion
  33.4 0.0 copy-done.4
  33.4 9.0 %all_gather.54 = bf16[16,4096]{1,0:T(8,128)(2,1)S(1)} all-gather(bf16[16,512]{1,0:T(8,128)(2,1)S(1)} %copy-done.4), channel_id=1, replica_groups=mesh['dp'=4,'tensor'=8] {'tensor'}, dimensions={1}, use_global_device_ids=true | all-gather | bytes 147456 | tf_op jit(solution)/shard_map/all_gather | solution.py:40
  42.4 15.5 %all_gather.55 = bf16[64,4096]{1,0:T(8,128)(2,1)S(1)} all-gather(bf16[16,4096]{1,0:T(8,128)(2,1)S(1)} %all_gather.54), channel_id=1, replica_groups=mesh['dp'=4,'tensor'=8] {'dp'}, dimensions={0}, use_global_device_ids=true | all-gather | bytes 655360 | tf_op jit(solution)/shard_map/all_gather | solution.py:46
  57.9 1.7 %gather_fusion.1 = bf16[64,4096]{1,0:T(8,128)(2,1)} fusion(bf16[64,4096]{1,0:T(8,128)(2,1)S(1)} %all_gather.55, s32[1024]{0:T(1024)S(1)} %pad_clamp_fusion), kind=kCustom, calls=%fused_computation.1 | custom fusion | bytes 1048832 | tf_op jit(solution)/shard_map/gather | solution.py:47
  59.6 0.0 copy-start.2
  59.6 2.3 %fusion.33 = (f32[64]{0:T(128)S(1)}, f32[64,256]{1,0:T(8,128)S(1)}) fusion(bf16[64,4096]{1,0:T(8,128)(2,1)} %gather_fusion.1, bf16[4096,256]{1,0:T(8,128)(2,1)} %param.13), kind=kOutput, calls=%fused_computation.73 | convolution fusion | flops 134234048 | bytes 2687232 | tf_op jit(solution)/shard_map/dot_general | solution.py:48
  61.9 0.3 multiply_reduce_fusion
  62.2 0.3 dynamic-update-slice.3
  62.5 0.3 dynamic-update-slice.4
  62.8 0.3 dynamic-update-slice.5
  63.0 0.3 dynamic-update-slice.6
  63.3 0.3 dynamic-update-slice.1
  63.6 0.3 dynamic-update-slice
  63.8 0.3 dynamic-update-slice.2
  64.1 40.1 %all-reduce.7 = (f32[2048]{0:T(1024)S(1)}, f32[2048]{0:T(1024)S(1)}, f32[2048]{0:T(1024)S(1)}, f32[2048]{0:T(1024)S(1)}, f32[2048]{0:T(1024)S(1)}, /*index=5*/f32[2048]{0:T(1024)S(1)}, f32[2048]{0:T(1024)S(1)}) all-reduce(f32[2048]{0:T(1024)S(1)} %dynamic-update-slice, ...), channel_id=2, replica_groups=mesh['dp'=4,'tensor'=8] {'dp','tensor'}, use_global_device_ids=true, to_apply=%add | all-reduce | flops 14336 | bytes 114688
  104.2 0.1 reshape.131
  104.3 0.1 reshape.132
  104.3 0.1 reshape.133
  104.4 0.1 reshape.134
  104.5 0.1 reshape.135
  104.5 0.1 reshape.136
  104.6 0.1 reshape.137
  104.7 3.5 %while.27 = (s32[]{:T(128)}, f32[64]{0:T(128)S(1)}, f32[64]{0:T(128)S(1)}, f32[64]{0:T(128)S(1)}, f32[64]{0:T(128)S(1)}, /*index=5*/f32[64]{0:T(128)S(1)}, f32[6...) while((s32[]{:T(128)}, f32[64]{0:T(128)S(1)}, ...), condition=%wide.region_9.10_spmd, body=%wide.region_8.9_spmd.sunk | while | flops 1221 | bytes 6875 | solution.py:16
  108.2 0.0 copy-done.2
  108.2 0.7 fusion.31
  108.9 5.1 %subtract_select_fusion = (f32[64]{0:T(128)S(1)}, pred[64]{0:T(512)(128)(4,1)S(1)}, f32[64]{0:T(128)S(1)}, f32[64]{0:T(128)S(1)}) fusion(f32[64]{0:T(128)S(1)} %get-tuple-element.367, f32[64]{0:T(128)S(1)} %get-tuple-element.366, s32[]{:T(128)} %bitcast.15, s32[]{:T(128)} %bitcast.14, s32[]{:T(128)} %bitcast.13, s32[]{:T(128)} %bitcast.12, s32[]{:T(128)} %bitcast.11, ...), kind=kLoop, calls=%fused_computation.64 | loop fusion | flops 2432 | bytes 2400 | tf_op jit(solution)/shard_map/mul | solution.py:104
  114.0 0.7 multiply_convert_fusion
  114.7 0.6 dynamic_slice.76
  115.3 0.6 dynamic_slice.77
  (146 shorter events, 2.5 us)
Async XLA Ops:
  0.6 31.2 %copy-start = (bf16[5120,256]{1,0:T(8,128)(2,1)S(1)}, bf16[5120,256]{1,0:T(8,128)(2,1)}, u32[]{:S(2)}) copy-start(bf16[5120,256]{1,0:T(8,128)(2,1)} %param.12) | copy-start | bytes 7864324
  0.6 31.2 %copy-start.3 = (f32[5120]{0:T(1024)S(1)}, f32[5120]{0:T(1024)}, u32[]{:S(2)}) copy-start(f32[5120]{0:T(1024)} %param.14) | copy-start | bytes 61444
  31.6 1.0 copy-start.1
  31.8 1.6 %copy-start.4 = (bf16[16,512]{1,0:T(8,128)(2,1)S(1)}, bf16[16,512]{1,0:T(8,128)(2,1)}, u32[]{:S(2)}) copy-start(bf16[16,512]{1,0:T(8,128)(2,1)} %param.11) | copy-start | bytes 49156
  59.6 48.6 %copy-start.2 = (s32[8]{0:T(128)S(1)}, s32[8]{0:T(128)}, u32[]{:S(2)}) copy-start(s32[8]{0:T(128)} %param.15) | copy-start | bytes 100
where the time goes:
time: 116 us
  blocking collectives  94 us (81%)
  other arithmetic  8.71 us (8%)
  local copies, waits for them, and re-layouts  8.31 us (7%)
  matrix products  3.05 us (3%)
    unnamed x1, blocking collectives  40.1 us
    all_gather x1, blocking collectives, on_device(): lax.all_gather(teacher_full, 'dp', axis=0, tiled=True).astype(jnp.float32)  18.4 us
    all_gather x1, blocking collectives, on_device(): student_all = lax.all_gather(student_full, 'dp', axis=0, tiled=True)  15.5 us
    all_gather x1, blocking collectives, on_device(): lax.all_gather(teacher_hidden, 'tensor', axis=1, tiled=True)  11 us
    all_gather x1, blocking collectives, on_device(): lax.all_gather(student_hidden, 'tensor', axis=1, tiled=True)  9.03 us
    mul x1, other arithmetic, on_device(): live_all * (picked_student - student_lse - (picked_teacher - teacher_lse))  5.07 us
    gather x2, local copies, waits for them, and re-layouts, on_device(): chosen_rows = student_all[student_row[token_ids]]  2.44 us
    dot_general x1, matrix products, on_device(): jnp.dot(chosen_rows, student_head, preferred_element_type=jnp.float32)  2.34 us

commit v1 on v0

--- a/solution.py
+++ b/solution.py
@@ -4,6 +4,11 @@
 from jax.sharding import PartitionSpec as P
 
 SLOT = 8
+
+
+def stack_and_merge(array, axis, d):
+    shards = lax.all_gather(array, axis)
+    return jnp.concatenate(shards, axis=d)
 
 
 def merged_2(array, axis, combine):
@@ -36,7 +41,7 @@
     token_ids = jnp.arange(token_count, dtype=jnp.int32)
     live_all = (token_ids % SLOT < lengths[token_ids // SLOT]).astype(jnp.float32)
     teacher_full, student_full = (
-        lax.all_gather(teacher_hidden, "tensor", axis=1, tiled=True),
+        stack_and_merge(teacher_hidden, "tensor", 1),
         lax.all_gather(student_hidden, "tensor", axis=1, tiled=True),
     )
     values = lax.all_gather(teacher_full, "dp", axis=0, tiled=True).astype(jnp.float32)

time: 116 us -> 116 us (level)
  no operation moved by 1% of the time
where the time goes in v1:
time: 116 us
  blocking collectives  94 us (81%)
  other arithmetic  8.71 us (8%)
  local copies, waits for them, and re-layouts  8.33 us (7%)
  matrix products  3.05 us (3%)
    unnamed x1, blocking collectives  40.1 us
    all_gather x1, blocking collectives, on_device(): lax.all_gather(teacher_full, 'dp', axis=0, tiled=True).astype(jnp.float32)  18.4 us
    all_gather x1, blocking collectives, on_device(): student_all = lax.all_gather(student_full, 'dp', axis=0, tiled=True)  15.5 us
    all_gather x1, blocking collectives, stack_and_merge(): shards = lax.all_gather(array, axis)  10.9 us
    all_gather x1, blocking collectives, on_device(): lax.all_gather(student_hidden, 'tensor', axis=1, tiled=True)  9.03 us
    mul x1, other arithmetic, on_device(): live_all * (picked_student - student_lse - (picked_teacher - teacher_lse))  5.07 us
    gather x2, local copies, waits for them, and re-layouts, on_device(): chosen_rows = student_all[student_row[token_ids]]  2.44 us
    dot_general x1, matrix products, on_device(): jnp.dot(chosen_rows, student_head, preferred_element_type=jnp.float32)  2.34 us

profile of v1, /device:TPU:0, one launch (start us, length us, event | category | flops | bytes accessed | tf_op | source)
XLA Modules:
  0.0 115.9 jit_solution(2874300564983139461)
XLA Ops:
  0.6 0.0 copy-start
  0.6 0.0 copy-start.3
  0.7 1.6 %gather_fusion.2 = s32[64]{0:T(128)S(1)} fusion(s32[64]{0:T(128)} %param.17, s32[1024]{0:T(1024)S(1)} %pad_clamp_fusion.1), kind=kCustom, calls=%fused_computation.2 | custom fusion | bytes 768 | tf_op jit(solution)/shard_map/gather | solution.py:54
  2.3 10.9 %all-gather = bf16[128,640]{1,0:T(8,128)(2,1)S(1)} all-gather(bf16[16,640]{1,0:T(8,128)(2,1)} %param.10), channel_id=2, replica_groups=mesh['dp'=4,'tensor'=8] {'tensor'}, dimensions={0}, use_global_device_ids=true | all-gather | bytes 184320 | tf_op jit(solution)/shard_map/all_gather | solution.py:10
  13.2 18.4 %all_gather.61 = bf16[64,5120]{1,0:T(8,128)(2,1)S(1)} all-gather(bf16[16,5120]{1,0:T(8,128)(2,1)S(1)} %bitcast.82), channel_id=1, replica_groups=mesh['dp'=4,'tensor'=8] {'dp'}, dimensions={0}, use_global_device_ids=true | all-gather | bytes 819200 | tf_op jit(solution)/shard_map/all_gather | solution.py:47
  31.6 0.0 copy-start.1
  31.6 0.2 fusion.17
  31.9 0.0 copy-start.4
  31.9 0.0 copy-done
  31.9 0.0 copy-done.3
  31.9 0.7 fusion.32
  32.6 0.0 copy-done.1
  32.6 0.8 gather_fusion
  33.4 0.0 copy-done.4
  33.4 9.0 %all_gather.57 = bf16[16,4096]{1,0:T(8,128)(2,1)S(1)} all-gather(bf16[16,512]{1,0:T(8,128)(2,1)S(1)} %copy-done.4), channel_id=1, replica_groups=mesh['dp'=4,'tensor'=8] {'tensor'}, dimensions={1}, use_global_device_ids=true | all-gather | bytes 147456 | tf_op jit(solution)/shard_map/all_gather | solution.py:45
  42.4 15.5 %all_gather.58 = bf16[64,4096]{1,0:T(8,128)(2,1)S(1)} all-gather(bf16[16,4096]{1,0:T(8,128)(2,1)S(1)} %all_gather.57), channel_id=1, replica_groups=mesh['dp'=4,'tensor'=8] {'dp'}, dimensions={0}, use_global_device_ids=true | all-gather | bytes 655360 | tf_op jit(solution)/shard_map/all_gather | solution.py:51
  57.9 1.7 %gather_fusion.1 = bf16[64,4096]{1,0:T(8,128)(2,1)} fusion(bf16[64,4096]{1,0:T(8,128)(2,1)S(1)} %all_gather.58, s32[1024]{0:T(1024)S(1)} %pad_clamp_fusion), kind=kCustom, calls=%fused_computation.1 | custom fusion | bytes 1048832 | tf_op jit(solution)/shard_map/gather | solution.py:52
  59.6 0.0 copy-start.2
  59.6 2.3 %fusion.33 = (f32[64]{0:T(128)S(1)}, f32[64,256]{1,0:T(8,128)S(1)}) fusion(bf16[64,4096]{1,0:T(8,128)(2,1)} %gather_fusion.1, bf16[4096,256]{1,0:T(8,128)(2,1)} %param.13), kind=kOutput, calls=%fused_computation.73 | convolution fusion | flops 134234048 | bytes 2687232 | tf_op jit(solution)/shard_map/dot_general | solution.py:53
  62.0 0.3 multiply_reduce_fusion
  62.3 0.3 dynamic-update-slice.3
  62.5 0.3 dynamic-update-slice.4
  62.8 0.3 dynamic-update-slice.5
  63.1 0.3 dynamic-update-slice.6
  63.3 0.3 dynamic-update-slice.1
  63.6 0.3 dynamic-update-slice
  63.8 0.3 dynamic-update-slice.2
  64.1 40.1 %all-reduce.7 = (f32[2048]{0:T(1024)S(1)}, f32[2048]{0:T(1024)S(1)}, f32[2048]{0:T(1024)S(1)}, f32[2048]{0:T(1024)S(1)}, f32[2048]{0:T(1024)S(1)}, /*index=5*/f32[2048]{0:T(1024)S(1)}, f32[2048]{0:T(1024)S(1)}) all-reduce(f32[2048]{0:T(1024)S(1)} %dynamic-update-slice, ...), channel_id=3, replica_groups=mesh['dp'=4,'tensor'=8] {'dp','tensor'}, use_global_device_ids=true, to_apply=%add | all-reduce | flops 14336 | bytes 114688
  104.2 0.1 reshape.140
  104.3 0.1 reshape.141
  104.3 0.1 reshape.142
  104.4 0.1 reshape.143
  104.5 0.1 reshape.144
  104.6 0.1 reshape.145
  104.6 0.1 reshape.146
  104.8 3.5 %while.27 = (s32[]{:T(128)}, f32[64]{0:T(128)S(1)}, f32[64]{0:T(128)S(1)}, f32[64]{0:T(128)S(1)}, f32[64]{0:T(128)S(1)}, /*index=5*/f32[64]{0:T(128)S(1)}, f32[6...) while((s32[]{:T(128)}, f32[64]{0:T(128)S(1)}, ...), condition=%wide.region_9.10_spmd, body=%wide.region_8.9_spmd.sunk | while | flops 1221 | bytes 6875 | solution.py:21
  108.2 0.0 copy-done.2
  108.2 0.7 fusion.31
  108.9 5.1 %subtract_select_fusion = (f32[64]{0:T(128)S(1)}, pred[64]{0:T(512)(128)(4,1)S(1)}, f32[64]{0:T(128)S(1)}, f32[64]{0:T(128)S(1)}) fusion(f32[64]{0:T(128)S(1)} %get-tuple-element.367, f32[64]{0:T(128)S(1)} %get-tuple-element.366, s32[]{:T(128)} %bitcast.15, s32[]{:T(128)} %bitcast.14, s32[]{:T(128)} %bitcast.13, s32[]{:T(128)} %bitcast.12, s32[]{:T(128)} %bitcast.11, ...), kind=kLoop, calls=%fused_computation.64 | loop fusion | flops 2432 | bytes 2400 | tf_op jit(solution)/shard_map/mul | solution.py:109
  114.0 0.7 multiply_convert_fusion
  114.8 0.6 dynamic_slice.76
  115.3 0.6 dynamic_slice.77
  (147 shorter events, 2.5 us)
Async XLA Ops:
  0.6 31.2 %copy-start = (bf16[5120,256]{1,0:T(8,128)(2,1)S(1)}, bf16[5120,256]{1,0:T(8,128)(2,1)}, u32[]{:S(2)}) copy-start(bf16[5120,256]{1,0:T(8,128)(2,1)} %param.12) | copy-start | bytes 7864324
  0.6 31.2 %copy-start.3 = (f32[5120]{0:T(1024)S(1)}, f32[5120]{0:T(1024)}, u32[]{:S(2)}) copy-start(f32[5120]{0:T(1024)} %param.14) | copy-start | bytes 61444
  31.6 1.0 copy-start.1
  31.9 1.6 %copy-start.4 = (bf16[16,512]{1,0:T(8,128)(2,1)S(1)}, bf16[16,512]{1,0:T(8,128)(2,1)}, u32[]{:S(2)}) copy-start(bf16[16,512]{1,0:T(8,128)(2,1)} %param.11) | copy-start | bytes 49156
  59.6 48.6 %copy-start.2 = (s32[8]{0:T(128)S(1)}, s32[8]{0:T(128)}, u32[]{:S(2)}) copy-start(s32[8]{0:T(128)} %param.15) | copy-start | bytes 100
